TPU v7x, 128 devices: a whole 4x4x4 slice. The times are simulated.
128 devices in a mesh: row: 8 (over y, z_lo), col: 16 (over x, z_hi, core).
Axes of the slice: x: 4, y: 4, z: 4 (z_hi: 2, z_lo: 2; z = z_hi * 2 + z_lo), core: 2. Of those that a mesh axis runs over, the one named last changes fastest.
Arguments:
- returns: bfloat16 [32768, 256], P(('col', 'row')), may hold values from -6 to 6
- start_day: int32 [32768], P(('col', 'row')), may hold values from 0 to 127
- shrink_code: int32 [1], replicated, may hold values from 64 to 191
- weights: bfloat16 [32768, 512], P(('col', 'row')), may hold values from -1.5 to 1.5
Outputs:
- exposures: float32 [32768, 512], P(('col', 'row'))
All inputs are finite; a program needn't handle non-finite values.
Results may differ from a plain program's by a relative error of at most 0.0041.
Values may be sent and summed in bfloat16 or wider, within the bound.
A program may use at most 128 MiB of HBM per device.

v0:
```python
import jax
import jax.numpy as jnp
from jax import lax
from jax.sharding import PartitionSpec as P

DENOM = 256


def square_bf(values):
    wide = values.astype(jnp.float32)
    return (wide * wide).astype(jnp.bfloat16)


def per_device(returns, start_day, shrink_code, weights):
    own_rows = returns.shape[0]
    num_days = returns.shape[1]
    days = jnp.arange(num_days, dtype=jnp.int32)
    listed = days[None, :] >= start_day[:, None]
    masked = jnp.where(listed, returns, jnp.zeros_like(returns))
    observed = (masked != 0).astype(jnp.bfloat16)
    squared = square_bf(masked)
    counts = jnp.sum(observed.astype(jnp.float32), axis=1)
    sigma = jnp.sqrt(
        jnp.sum(squared.astype(jnp.float32), axis=1) / jnp.maximum(counts, 1.0) + 1e-06
    )
    scaled = (sigma[:, None] * weights.astype(jnp.float32)).astype(jnp.bfloat16)
    delta = shrink_code[0].astype(jnp.float32) / DENOM
    col_y, col_v = (
        lax.all_gather(masked, "row", axis=0, tiled=True),
        lax.all_gather(scaled, "row", axis=0, tiled=True),
    )
    col_obs = (col_y != 0).astype(jnp.bfloat16)
    col_sq = square_bf(col_y)
    row_y = lax.all_gather(masked, "col", axis=0, tiled=True)
    ncol = lax.axis_size("col")
    my_row = lax.axis_index("row")
    my_col = lax.axis_index("col")
    width = col_y.shape[0]
    port_cols = col_v.shape[1]
    half_rows = own_rows // 2
    col_pos = jnp.arange(width, dtype=jnp.int32)
    local_pos = jnp.arange(own_rows, dtype=jnp.int32)
    diag_ident = (col_pos[None, :] == my_row * own_rows + local_pos[:, None]).astype(jnp.float32)

    def shrink(rows_y, cols_y, cols_obs, cols_sq, ident):
        rows_o = (rows_y != 0).astype(jnp.bfloat16)
        rows_s = square_bf(rows_y)
        cross = jnp.dot(rows_y, cols_y.T, preferred_element_type=jnp.float32)
        left = jnp.dot(rows_s, cols_obs.T, preferred_element_type=jnp.float32)
        right = jnp.dot(rows_o, cols_sq.T, preferred_element_type=jnp.float32)
        corr = cross / jnp.sqrt(left * right + 1e-06)
        return ((1.0 - delta) * corr + delta * ident).astype(jnp.bfloat16)

    def piece_rows(piece):
        return lax.dynamic_slice_in_dim(row_y, piece * own_rows, own_rows, 0)

    row_v = lax.all_gather(scaled, "col", axis=0, tiled=True)
    half = ncol // 2
    diag_shrunk = shrink(piece_rows(my_col), col_y, col_obs, col_sq, diag_ident)
    diag_term = jnp.dot(diag_shrunk, col_v, preferred_element_type=jnp.float32)
    empty_terms = jnp.zeros((ncol * own_rows, port_cols), jnp.float32)
    terms = lax.dynamic_update_slice_in_dim(empty_terms, diag_term, my_col * own_rows, 0)

    def add_rows(buffer, first, extra):
        older = lax.dynamic_slice_in_dim(buffer, first, own_rows, 0)
        return lax.dynamic_update_slice_in_dim(buffer, older + extra, first, 0)

    def step(dist, carry):
        buffer, col_acc = carry
        piece = (my_col + ncol - dist) % ncol
        first = piece * own_rows
        shrunk = shrink(piece_rows(piece), col_y, col_obs, col_sq, 0.0)
        term = jnp.dot(shrunk, col_v, preferred_element_type=jnp.float32)
        piece_v = lax.dynamic_slice_in_dim(row_v, first, own_rows, 0)
        mirror = jnp.dot(shrunk.T, piece_v, preferred_element_type=jnp.float32)
        return (add_rows(buffer, first, term), col_acc + mirror)

    start_acc = jnp.zeros((width, port_cols), jnp.float32)
    terms, col_acc = lax.fori_loop(1, half, step, (terms, start_acc))
    opposite = (my_col + half) % ncol
    opp_first = opposite * own_rows
    opp_y = piece_rows(opposite)
    opp_v = lax.dynamic_slice_in_dim(row_v, opp_first, own_rows, 0)
    groups = width // own_rows
    upper_y = col_y.reshape(groups, own_rows, num_days)[:, half_rows:].reshape(-1, num_days)
    upper_obs = col_obs.reshape(groups, own_rows, num_days)[:, half_rows:].reshape(-1, num_days)
    upper_sq = col_sq.reshape(groups, own_rows, num_days)[:, half_rows:].reshape(-1, num_days)
    upper_v = col_v.reshape(groups, own_rows, port_cols)[:, half_rows:].reshape(-1, port_cols)

    def lower_side(unused):
        shrunk = shrink(opp_y[:half_rows], col_y, col_obs, col_sq, 0.0)
        term = jnp.dot(shrunk, col_v, preferred_element_type=jnp.float32)
        padding = jnp.zeros((own_rows - half_rows, port_cols), jnp.float32)
        mirror = jnp.dot(shrunk.T, opp_v[:half_rows], preferred_element_type=jnp.float32)
        return (jnp.concatenate([term, padding], axis=0), mirror)

    def upper_side(unused):
        shrunk = shrink(opp_y, upper_y, upper_obs, upper_sq, 0.0)
        term = jnp.dot(shrunk, upper_v, preferred_element_type=jnp.float32)
        mirror_hi = jnp.dot(shrunk.T, opp_v, preferred_element_type=jnp.float32)
        mirror_hi = mirror_hi.reshape(groups, own_rows - half_rows, port_cols)
        padding = jnp.zeros((groups, half_rows, port_cols), jnp.float32)
        mirror = jnp.concatenate([padding, mirror_hi], axis=1).reshape(width, port_cols)
        return (term, mirror)

    opp_term, opp_mirror = lax.cond(my_col < opposite, lower_side, upper_side, 0)
    terms = add_rows(terms, opp_first, opp_term)
    col_acc = col_acc + opp_mirror
    col_part = lax.psum_scatter(col_acc, "row", scatter_dimension=0, tiled=True)
    row_part = lax.psum_scatter(terms, "col", scatter_dimension=0, tiled=True)
    total = row_part + col_part
    return sigma[:, None] * total


def solution(mesh):
    in_specs = (P(("col", "row"), None), P(("col", "row")), P(), P(("col", "row"), None))
    out_specs = P(("col", "row"), None)
    return jax.shard_map(
        per_device, mesh=mesh, in_specs=in_specs, out_specs=out_specs, check_vma=False
    )
```

profile of v0, /device:TPU:0, one launch (start us, length us, event | category | flops | bytes accessed | tf_op | source)
XLA Modules:
  0.0 521.0 jit_solution(7496719435716008836)
XLA Ops:
  9.1 1.8 multiply_convert_fusion.7
  12.2 38.1 %all-gather.7.cloned.1.call-done = bf16[2048,256]{1,0:T(8,128)(2,1)} async-done(((bf16[256,256]{1,0:T(8,128)(2,1)}), bf16[2048,256]{1,0:T(8,128)(2,1)}) %all-gather.7.cloned.1.call-update) | async-done | bytes 1048592 | tf_op jit(solution)/shard_map/all_gather | solution.py:29
  53.1 47.5 %all-gather.5.cloned.1.call-done = bf16[4096,256]{1,0:T(8,128)(2,1)} async-done(((bf16[256,256]{1,0:T(8,128)(2,1)}), bf16[4096,256]{1,0:T(8,128)(2,1)}) %all-gather.5.cloned.1.call-update) | async-done | bytes 2097168 | tf_op jit(solution)/shard_map/all_gather | solution.py:34
  101.6 2.8 fusion.59
  104.4 2.7 fusion.68
  107.1 45.2 %all-gather.9.cloned.1.call-done = bf16[2048,512]{1,0:T(8,128)(2,1)} async-done(((bf16[256,512]{1,0:T(8,128)(2,1)}), bf16[2048,512]{1,0:T(8,128)(2,1)}) %all-gather.9.cloned.1.call-update) | async-done | bytes 2097168 | tf_op jit(solution)/shard_map/all_gather | solution.py:30
  152.2 4.3 broadcast_in_dim.4
  156.5 5.0 fusion.53
  161.5 50.0 %all-gather.11.cloned.1.call-done = bf16[4096,512]{1,0:T(8,128)(2,1)} async-done(((bf16[256,512]{1,0:T(8,128)(2,1)}), bf16[4096,512]{1,0:T(8,128)(2,1)}) %all-gather.11.cloned.1.call-update) | async-done | bytes 4194320 | tf_op jit(solution)/shard_map/all_gather | solution.py:57
  211.5 87.2 %while.18 = (s32[]{:T(128)}, f32[4096,512]{1,0:T(8,128)}, f32[2048,512]{1,0:T(8,128)}, s32[]{:T(128)}, f32[]{:T(128)}, /*index=5*/bf16[4096,256]{1,0:T(8,128)(2,...) while((s32[]{:T(128)}, f32[4096,512]{1,0:T(8,128)}, ...), condition=%wide.region_3.4_spmd.clone, body=%wide.region_2.3_spmd.clone.sunk | while | flops 1884815360 | bytes 31065484 | solution.py:79
  216.0 3.2 fusion.133
  219.3 3.6 select_add_fusion.2
  227.4 3.2 fusion.133
  230.6 4.9 select_add_fusion.2
  240.0 3.2 fusion.133
  243.2 4.9 select_add_fusion.2
  252.6 3.2 fusion.133
  255.8 4.9 select_add_fusion.2
  265.3 3.2 fusion.133
  268.5 4.9 select_add_fusion.2
  277.9 3.2 fusion.133
  281.1 4.9 select_add_fusion.2
  290.6 3.2 fusion.133
  293.8 4.9 select_add_fusion.2
  299.7 10.4 %conditional.1 = (f32[256,512]{1,0:T(8,128)}, f32[2048,512]{1,0:T(8,128)}) conditional(s32[]{:T(128)} %convert_element_type.115, (f32[]{:T(128)}, bf16[2048,256]{1,0:T(8,128)(2,1)S(1)}, bf16[256,256]{1,0:T(8,128)(2,1)S(1)}, bf16[2048,256]{1,0:T(8,128)(2,1)S(1)}, bf16[2048,256]{1,0:T(8,128)(2,1)}, /*index=5*/bf16[2048,512]{1,0:T(8,128)(2,1)}, ...), branch_computations={%region_4.5_spmd, %region_5.6_spmd} | conditional | flops 941359104 | bytes 24969324 | solution.py:106
  304.4 2.7 fusion.16
  307.1 2.1 fusion.85
  310.0 6.4 %add.193 = f32[2048,512]{1,0:T(8,128)} add(f32[2048,512]{1,0:T(8,128)} %get-tuple-element.338, f32[2048,512]{1,0:T(8,128)} %get-tuple-element.339) | non-fusion elementwise | flops 1048576 | bytes 12582912 | tf_op jit(solution)/shard_map/add | solution.py:108
  316.5 2.1 add_dynamic-update-slice_fusion
  318.6 85.8 %reduce-scatter.5.cloned.1.call-done = f32[256,512]{1,0:T(8,128)} async-done(((f32[2048,512]{1,0:T(8,128)}), f32[256,512]{1,0:T(8,128)}) %reduce-scatter.5.cloned.1.call-update) | async-done | bytes 524304 | tf_op jit(solution)/shard_map/reduce_scatter | solution.py:109
  404.4 107.6 %reduce-scatter.3.cloned.1.call-done = f32[256,512]{1,0:T(8,128)} async-done(((f32[4096,512]{1,0:T(8,128)}), f32[256,512]{1,0:T(8,128)}) %reduce-scatter.3.cloned.1.call-update) | async-done | bytes 524304 | tf_op jit(solution)/shard_map/reduce_scatter | solution.py:110
  512.0 2.1 add_multiply_fusion
  (65 shorter events, 44.7 us)
Async XLA Ops:
  6.5 43.8 %all-gather.7.cloned.1.call-start = ((), (), s32[]{:S(2)}) async-start(), calls=%async_computation.3 | async-start | bytes 1179648 | tf_op jit(solution)/shard_map/all_gather | solution.py:29
  8.2 92.4 %all-gather.5.cloned.1.call-start = ((), (), s32[]{:S(2)}) async-start(), calls=%async_computation.2 | async-start | bytes 2228224 | tf_op jit(solution)/shard_map/all_gather | solution.py:34
  9.0 143.2 %all-gather.9.cloned.1.call-start = ((), (), s32[]{:S(2)}) async-start(), calls=%async_computation.4 | async-start | bytes 2359296 | tf_op jit(solution)/shard_map/all_gather | solution.py:30
  10.8 200.7 %all-gather.11.cloned.1.call-start = ((), (), s32[]{:S(2)}) async-start(), calls=%async_computation.5 | async-start | bytes 4456448 | tf_op jit(solution)/shard_map/all_gather | solution.py:57
  11.4 393.0 %reduce-scatter.5.cloned.1.call-start = ((), (), s32[]{:S(2)}) async-start(), calls=%async_computation.7 | async-start | bytes 4718592 | tf_op jit(solution)/shard_map/reduce_scatter | solution.py:109
  50.3 1.6 copy-start
  212.9 1.5 copy-start.1
  224.2 1.5 copy-start.1
  236.9 1.5 copy-start.1
  249.5 1.5 copy-start.1
  262.1 1.5 copy-start.1
  274.8 1.5 copy-start.1
  287.4 1.5 copy-start.1
  299.7 3.0 copy-start.2
  301.2 1.5 copy-start.3
  316.5 195.5 %reduce-scatter.3.cloned.1.call-start = ((), (), s32[]{:S(2)}) async-start(), calls=%async_computation.6 | async-start | bytes 8912896 | tf_op jit(solution)/shard_map/reduce_scatter | solution.py:110
Sparse Core Ops, SparseCore 0:
  9.0 41.2 all-gather.6
  52.7 47.9 all-gather.4
  102.3 49.8 all-gather.8
  154.5 56.9 all-gather.10
  316.6 87.7 reduce-scatter.4
  408.6 103.3 reduce-scatter.2
where the time goes:
time: 522 us; the launch traced here: 521 us
  waiting for transfers between devices  375 us (72%)
  matrix products  107 us (20%)
  other arithmetic  16.9 us (3%)
  between operations  14.2 us (3%)
  local copies, waits for them, and re-layouts  7.06 us (1%)
    reduce_scatter x1, waiting for transfers between devices, per_device(): row_part = lax.psum_scatter(terms, 'col', scatter_dimension=0, tiled=True)  108 us
    reduce_scatter x1, waiting for transfers between devices, per_device(): col_part = lax.psum_scatter(col_acc, 'row', scatter_dimension=0, tiled=True)  85.8 us
    all_gather x1, waiting for transfers between devices, per_device(): row_v = lax.all_gather(scaled, 'col', axis=0, tiled=True)  50 us
    all_gather x1, waiting for transfers between devices, per_device(): row_y = lax.all_gather(masked, 'col', axis=0, tiled=True)  47.5 us
    all_gather x1, waiting for transfers between devices, per_device(): lax.all_gather(scaled, 'row', axis=0, tiled=True)  45.2 us
    all_gather x1, waiting for transfers between devices, per_device(): lax.all_gather(masked, 'row', axis=0, tiled=True)  38.1 us
    dot_general x7, matrix products, step(): mirror = jnp.dot(shrunk.T, piece_v, preferred_element_type=jnp.float32)  33.3 us
    dot_general x7, matrix products, step(): term = jnp.dot(shrunk, col_v, preferred_element_type=jnp.float32)  22.4 us
  transfers between devices with their start and end apart: 6, of which 6 were waited for; matrix products, arithmetic and copies ran while one was open for 4% of the time, Pallas kernels for 0%

commit v1 on v0

v1 whole, which is shorter than its diff:
```python
import functools

import jax
import jax.numpy as jnp
from jax import lax
from jax.experimental import pallas as pl
from jax.experimental.pallas import tpu as pltpu
from jax.sharding import PartitionSpec as P

DENOM = 256
MESH = pl.DeviceIdType.MESH
NT = (((1,), (1,)), ((), ()))
F32 = jnp.float32
BF16 = jnp.bfloat16


def flip1(v):
    return v + 1 - 2 * lax.rem(v, 2)


def flip3(v):
    return 3 - v


def peers():
    row = lax.axis_index("row")
    col = lax.axis_index("col")
    y, zl = lax.div(row, 2), lax.rem(row, 2)
    x, zh, core = lax.div(col, 4), lax.rem(lax.div(col, 2), 2), lax.rem(col, 2)
    z = zh * 2 + zl

    def device(x, y, z, core):
        return (y * 2 + lax.rem(z, 2), (x * 2 + lax.div(z, 2)) * 2 + core)

    def pick(first, second):
        return tuple(a * (1 - core) + b * core for a, b in zip(first, second))

    out = []
    for flip in (flip1, flip3):
        along_x = device(flip(x), y, z, core)
        along_y = device(x, flip(y), z, core)
        along_z = device(x, y, flip(z), core)
        out.append([pick(along_x, along_z), along_y, pick(along_z, along_x)])
    return out[0], out[1], device(x, y, z, 1 - core)


def kernel(
    ret_ref, start_ref, code_ref, w_ref, out_ref,
    yr, orow, srow, yc, oc, sc, v, s, diag, sig,
    sbuf, rbuf2, rbuf1, rbuf0,
    yc_send, yc_recv, yp_send, yp_recv, yr_send, yr_recv,
    v_send, v_recv, vp_send, vp_recv, o_send, o_recv,
):
    nb, days = ret_ref.shape
    half = w_ref.shape[1] // 2
    cbits, rbits, mate = peers()

    barrier = pltpu.get_barrier_semaphore()
    for peer in (*cbits, *rbits, mate):
        pl.semaphore_signal(barrier, inc=1, device_id=peer, device_id_type=MESH)

    starts = start_ref[...].reshape(1, nb).astype(F32)
    day = lax.broadcasted_iota(jnp.int32, (days, nb), 0).astype(F32)
    listed = jnp.where(day >= starts, 1.0, 0.0).astype(F32).T
    masked = jnp.where(listed > 0.5, ret_ref[...].astype(F32), 0.0)
    seen = jnp.where(masked != 0.0, 1.0, 0.0)
    squared = (masked * masked).astype(BF16).astype(F32)
    counts = jnp.sum(seen, axis=1, keepdims=True)
    sigma = jnp.sqrt(
        jnp.sum(squared, axis=1, keepdims=True) / jnp.maximum(counts, 1.0) + 1e-06
    )
    yr[0:nb, :] = masked.astype(BF16)
    yc[0:nb, :] = masked.astype(BF16)
    scaled = (sigma * w_ref[...].astype(F32)).astype(BF16)
    v[0, 0:nb, :] = scaled[:, :half]
    v[1, 0:nb, :] = scaled[:, half:]
    sig[...] = jnp.broadcast_to(sigma, sig.shape)
    delta = code_ref[0].astype(F32) / DENOM
    keep = 1.0 - delta

    pl.semaphore_wait(barrier, 7)

    def rows(pos, count=1):
        return pl.ds(pos * nb, count * nb)

    def yc_copy(m, bit):
        to = m + (1 << bit)
        return pltpu.make_async_remote_copy(
            src_ref=yc.at[rows(2 * m)], dst_ref=yc.at[rows(2 * to)],
            send_sem=yc_send.at[to], recv_sem=yc_recv.at[to],
            device_id=cbits[bit], device_id_type=MESH)

    def yp_copy(m):
        return pltpu.make_async_remote_copy(
            src_ref=yc.at[rows(2 * m)], dst_ref=yc.at[rows(2 * m + 1)],
            send_sem=yp_send.at[m], recv_sem=yp_recv.at[m],
            device_id=mate, device_id_type=MESH)

    def yr_copy(m, bit):
        to = m + (1 << bit)
        return pltpu.make_async_remote_copy(
            src_ref=yr.at[rows(m)], dst_ref=yr.at[rows(to)],
            send_sem=yr_send.at[to], recv_sem=yr_recv.at[to],
            device_id=rbits[bit], device_id_type=MESH)

    def v_copy(h, m, bit):
        to = m + (1 << bit)
        return pltpu.make_async_remote_copy(
            src_ref=v.at[h, rows(2 * m)], dst_ref=v.at[h, rows(2 * to)],
            send_sem=v_send.at[h, to], recv_sem=v_recv.at[h, to],
            device_id=cbits[bit], device_id_type=MESH)

    def vp_copy(h, m):
        return pltpu.make_async_remote_copy(
            src_ref=v.at[h, rows(2 * m)], dst_ref=v.at[h, rows(2 * m + 1)],
            send_sem=vp_send.at[h, m], recv_sem=vp_recv.at[h, m],
            device_id=mate, device_id_type=MESH)

    def bits_above(m):
        return [b for b in range(3) if (1 << b) > m]

    def last_bit(m):
        return m.bit_length() - 1

    def arrive(copy, m, forward):
        if m:
            b = last_bit(m)
            copy(m - (1 << b), b).wait_recv()
        for b in reversed(bits_above(m)):
            copy(m, b).start()
        if forward is not None:
            forward(m).start()

    def y_arrive(m):
        arrive(yc_copy, m, yp_copy)

    def r_arrive(m):
        arrive(yr_copy, m, None)

    def v_arrive(h, m):
        arrive(functools.partial(v_copy, h), m, functools.partial(vp_copy, h))

    def derive(y_ref, o_ref, s_ref, pos, count):
        def body(i, carry):
            r = pl.ds(pl.multiple_of((pos + i) * nb, nb), nb)
            y = y_ref[r, :]
            o_ref[r, :] = jnp.where(y != 0, 1.0, 0.0).astype(BF16)
            wide = y.astype(F32)
            s_ref[r, :] = (wide * wide).astype(BF16)
            return carry
        lax.fori_loop(0, count, body, 0)

    def corr_tile(r, c):
        cross = lax.dot_general(yr[r, :], yc[c, :], NT, preferred_element_type=F32)
        left = lax.dot_general(srow[r, :], oc[c, :], NT, preferred_element_type=F32)
        right = lax.dot_general(orow[r, :], sc[c, :], NT, preferred_element_type=F32)
        return cross * lax.rsqrt(left * right + 1e-06) * keep

    def corr_tiles(rpos, cchip, count):
        r = pl.ds(rpos * nb, 4 * nb)

        def body(i, carry):
            c = pl.ds(pl.multiple_of((cchip + i) * 2 * nb, 2 * nb), 2 * nb)
            s[r, c] = corr_tile(r, c).astype(BF16)
            return carry
        lax.fori_loop(0, count, body, 0)

    def apply_rows(h, pos):
        r = pl.ds(pl.multiple_of(pos * nb, nb), nb)
        return jnp.dot(s[r, :], v[h], preferred_element_type=F32)

    def o2_copy(h, i):
        return pltpu.make_async_remote_copy(
            src_ref=sbuf.at[h, 4 + i], dst_ref=rbuf2.at[h, i],
            send_sem=o_send.at[h, 4 + i], recv_sem=o_recv.at[h, 4 + i],
            device_id=rbits[2], device_id_type=MESH)

    def o1_copy(h, i):
        return pltpu.make_async_remote_copy(
            src_ref=sbuf.at[h, 2 + i], dst_ref=rbuf1.at[h, i],
            send_sem=o_send.at[h, 2 + i], recv_sem=o_recv.at[h, 2 + i],
            device_id=rbits[1], device_id_type=MESH)

    def o0_copy(h):
        return pltpu.make_async_remote_copy(
            src_ref=sbuf.at[h, 1], dst_ref=rbuf0.at[h],
            send_sem=o_send.at[h, 1], recv_sem=o_recv.at[h, 1],
            device_id=rbits[0], device_id_type=MESH)

    def group4(h):
        def body(i, carry):
            sbuf[h, 4 + i] = apply_rows(h, 4 + i).astype(BF16)
            o2_copy(h, i).start()
            return carry
        lax.fori_loop(0, 4, body, 0)

    def group2(h):
        def body(i, carry):
            part = apply_rows(h, 2 + i)
            o2_copy(h, 2 + i).wait_recv()
            sbuf[h, 2 + i] = (part + rbuf2[h, 2 + i].astype(F32)).astype(BF16)
            o1_copy(h, i).start()
            return carry
        lax.fori_loop(0, 2, body, 0)

    def group1(h):
        part = apply_rows(h, 1)
        o2_copy(h, 1).wait_recv()
        part = part + rbuf2[h, 1].astype(F32)
        o1_copy(h, 1).wait_recv()
        sbuf[h, 1] = (part + rbuf1[h, 1].astype(F32)).astype(BF16)
        o0_copy(h).start()

    def group0(h):
        part = apply_rows(h, 0)
        o2_copy(h, 0).wait_recv()
        part = part + rbuf2[h, 0].astype(F32)
        o1_copy(h, 0).wait_recv()
        out_ref[:, h * half:(h + 1) * half] = part + rbuf1[h, 0].astype(F32)

    def finish(h):
        o0_copy(h).wait_recv()
        cols = slice(h * half, (h + 1) * half)
        out_ref[:, cols] = (out_ref[:, cols] + rbuf0[h].astype(F32)) * sig[:, 0:1]

    y_arrive(0)
    r_arrive(0)
    derive(yr, orow, srow, 0, 1)
    derive(yc, oc, sc, 0, 1)
    own = rows(0)
    ident = (
        lax.broadcasted_iota(jnp.int32, (nb, nb), 0)
        == lax.broadcasted_iota(jnp.int32, (nb, nb), 1)
    ).astype(F32)
    diag[...] = (corr_tile(own, own) + delta * ident).astype(BF16)

    for m in (1, 2, 3):
        y_arrive(m)
        r_arrive(m)
    v_arrive(0, 0)
    derive(yr, orow, srow, 1, 3)
    for m in (0, 1, 2, 3):
        yp_copy(m).wait_recv()
    derive(yc, oc, sc, 1, 7)
    corr_tiles(0, 0, 4)
    s[0:nb, 0:nb] = diag[...]

    for m in (4, 5, 6, 7):
        y_arrive(m)
        r_arrive(m)
    for m in (1, 2, 3):
        v_arrive(0, m)
    v_arrive(1, 0)
    derive(yr, orow, srow, 4, 4)
    corr_tiles(4, 0, 4)
    for m in (4, 5, 6, 7):
        yp_copy(m).wait_recv()
    for m in (4, 5, 6, 7):
        v_arrive(0, m)
    for m in (1, 2, 3):
        v_arrive(1, m)
    derive(yc, oc, sc, 8, 8)
    corr_tiles(4, 4, 4)
    for m in range(8):
        vp_copy(0, m).wait_recv()
    group4(0)
    for m in (4, 5, 6, 7):
        v_arrive(1, m)
    corr_tiles(0, 4, 4)
    for m in range(8):
        vp_copy(1, m).wait_recv()
    group4(1)
    group2(0)
    group2(1)
    group1(0)
    group1(1)
    group0(0)
    group0(1)
    finish(0)
    finish(1)

    for to in range(1, 8):
        b = last_bit(to)
        m = to - (1 << b)
        yc_copy(m, b).wait_send()
        yr_copy(m, b).wait_send()
        for h in (0, 1):
            v_copy(h, m, b).wait_send()
    for m in range(8):
        yp_copy(m).wait_send()
        for h in (0, 1):
            vp_copy(h, m).wait_send()
    for h in (0, 1):
        for i in range(4):
            o2_copy(h, i).wait_send()
        for i in range(2):
            o1_copy(h, i).wait_send()
        o0_copy(h).wait_send()


def per_device(returns, start_day, shrink_code, weights):
    nb, days = returns.shape
    port = weights.shape[1]
    half = port // 2
    nr, nc = 8 * nb, 16 * nb
    vmem = pl.BlockSpec(memory_space=pltpu.VMEM)
    smem = pl.BlockSpec(memory_space=pltpu.SMEM)
    dma = pltpu.SemaphoreType.DMA
    return pl.pallas_call(
        kernel,
        out_shape=jax.ShapeDtypeStruct((nb, port), F32),
        in_specs=[vmem, vmem, smem, vmem],
        out_specs=vmem,
        scratch_shapes=[
            pltpu.VMEM((nr, days), BF16), pltpu.VMEM((nr, days), BF16), pltpu.VMEM((nr, days), BF16),
            pltpu.VMEM((nc, days), BF16), pltpu.VMEM((nc, days), BF16), pltpu.VMEM((nc, days), BF16),
            pltpu.VMEM((2, nc, half), BF16),
            pltpu.VMEM((nr, nc), BF16),
            pltpu.VMEM((nb, nb), BF16),
            pltpu.VMEM((nb, 128), F32),
            pltpu.VMEM((2, 8, nb, half), BF16),
            pltpu.VMEM((2, 4, nb, half), BF16),
            pltpu.VMEM((2, 2, nb, half), BF16),
            pltpu.VMEM((2, nb, half), BF16),
            dma((8,)), dma((8,)), dma((8,)), dma((8,)), dma((8,)), dma((8,)),
            dma((2, 8)), dma((2, 8)), dma((2, 8)), dma((2, 8)), dma((2, 8)), dma((2, 8)),
        ],
        compiler_params=pltpu.CompilerParams(
            collective_id=0, has_side_effects=True, vmem_limit_bytes=60 << 20
        ),
    )(returns, start_day.reshape(1, nb), shrink_code, weights)


def solution(mesh):
    in_specs = (P(("col", "row"), None), P(("col", "row")), P(), P(("col", "row"), None))
    out_specs = P(("col", "row"), None)
    return jax.shard_map(
        per_device, mesh=mesh, in_specs=in_specs, out_specs=out_specs, check_vma=False
    )
```

time: 522 us -> 74.9 us (0.14)
  waiting for transfers between devices: 375 us -> 0 us
  matrix products: 107 us -> 0 us
  Pallas kernels: 0 us -> 72.2 us
  other arithmetic: 16.9 us -> 0 us
  between operations: 14.2 us -> 0.66 us
    reduce_scatter x2 -> x0, waiting for transfers between devices: 193 us -> none  [the longest x1 108 us: per_device(): row_part = lax.psum_scatter(terms, 'col', scatter_dimension=0, tiled=True)]
    all_gather x4 -> x0, waiting for transfers between devices: 181 us -> none  [the longest x1 50 us: per_device(): row_v = lax.all_gather(scaled, 'col', axis=0, tiled=True)]
    dot_general x43 -> x0, matrix products: 107 us -> none  [the longest x7 33.3 us: step(): mirror = jnp.dot(shrunk.T, piece_v, preferred_element_type=jnp.float32)]
    pallas_call x0 -> x1, Pallas kernels: none -> 72.2 us  [per_device(): pl.pallas_call(kernel, out_shape=jax.ShapeDtypeStruct((nb, port), F32), i...]
    add x2 -> x0, other arithmetic: 6.44 us -> none  [the longest x1 6.44 us: per_device(): col_acc = col_acc + opp_mirror]
  transfers between devices with their start and end apart: 6 -> 0, of which waited for: 6 -> 0; matrix products, arithmetic and copies ran while one was open for 4% -> 0% of each run, Pallas kernels for 0% -> 0%
where the time goes in v1:
time: 74.9 us; the launch traced here: 74.7 us
  Pallas kernels  72.2 us (96%)
  local copies, waits for them, and re-layouts  1.87 us (2%)
    pallas_call x1, Pallas kernels, per_device(): pl.pallas_call(kernel, out_shape=jax.ShapeDtypeStruct((nb, port), F32), i...  72.2 us
    unnamed x1, local copies, waits for them, and re-layouts  1.87 us

profile of v1, /device:TPU:0, one launch (start us, length us, event | category | flops | bytes accessed | tf_op | source)
XLA Modules:
  0.0 74.7 jit_solution(691625021797679623)
XLA Ops:
  0.7 72.2 %shard_map.46 = f32[256,512]{1,0:T(8,128)} custom-call(bf16[256,256]{1,0:T(8,128)(2,1)} %ret_ref.1, s32[1,256]{1,0:T(1,128)} %bitcast.1, s32[1]{0:T(128)S(6)} %copy.6.code_ref, bf16[256,512]{1,0:T(8,128)(2,1)} %w_ref.1), custom_call_target="tpu_custom_call" | custom-call | tf_op jit(solution)/shard_map/pallas_call | solution.py:309
  72.9 1.9 %copy.7 = f32[256,512]{1,0:T(8,128)} copy(f32[256,512]{1,0:T(8,128)} %shard_map.46) | data formatting | bytes 1048576

commit v2 on v0

v2 whole, which is shorter than its diff:
```python
import functools

import jax
import jax.numpy as jnp
from jax import lax
from jax.experimental import pallas as pl
from jax.experimental.pallas import tpu as pltpu
from jax.sharding import PartitionSpec as P

DENOM = 256
MESH = pl.DeviceIdType.MESH
NT = (((1,), (1,)), ((), ()))
F32 = jnp.float32
BF16 = jnp.bfloat16

MASKS = (0, 1, 2, 4, 3, 5, 6, 7)
PLACE = tuple(MASKS.index(m) for m in range(8))

ORDERS = ((0, 1, 2), (1, 2, 0), (2, 0, 1), (2, 1, 0))
PLAN = (
    "s01", "s11", "s12", "y1", "r1", "r2", "y4", "s02", "v01", "y2", "T00",
    "v11", "v12", "T01",
    "r3", "v05", "y3", "y5", "T02",
    "s04", "v02", "T12",
    "v03", "m1", "s14", "T11",
    "v15", "y7", "y6", "T10",
    "v04", "v13", "T13",
    "v16", "v06", "v07", "m0", "T03",
    "A05",
    "v17", "v14", "o05", "A07",
    "o17", "o07", "A03",
    "o13", "o03", "A17",
    "o37", "o27", "A06",
    "o16", "A15",
    "o25", "o35", "A16",
    "o36", "o06", "A13",
    "o15", "A02",
    "o33", "o26", "A04",
    "o23", "A01",
    "o12", "o14", "A11",
    "o02", "o01", "o21", "A14",
    "o11", "A00",
    "A12",
    "o32", "o24", "o04", "o22", "A10",
    "o34", "o31", "o00", "o10", "o20", "o30",
)


def flip1(v):
    return v + 1 - 2 * lax.rem(v, 2)


def flip3(v):
    return 3 - v


def peers():
    row = lax.axis_index("row")
    col = lax.axis_index("col")
    y, zl = lax.div(row, 2), lax.rem(row, 2)
    x, zh, core = lax.div(col, 4), lax.rem(lax.div(col, 2), 2), lax.rem(col, 2)
    z = zh * 2 + zl

    def device(x, y, z, core):
        return (y * 2 + lax.rem(z, 2), (x * 2 + lax.div(z, 2)) * 2 + core)

    def pick(first, second):
        return tuple(a * (1 - core) + b * core for a, b in zip(first, second))

    out = []
    for flip in (flip1, flip3):
        along_x = device(flip(x), y, z, core)
        along_y = device(x, flip(y), z, core)
        along_z = device(x, y, flip(z), core)
        out.append([pick(along_x, along_z), along_y, pick(along_z, along_x)])
    return out[0], out[1], device(x, y, z, 1 - core)


def last_bit(m):
    return m.bit_length() - 1


def stage_of(q, m):
    for k, b in enumerate(ORDERS[q]):
        if m >> b & 1:
            return k
    return 3


def kernel(
    ret_ref, start_ref, code_ref, w_ref, out_ref,
    yr, orow, srow, yc, oc, sc, v, s, diag, sig, part, sbuf, rbuf,
    yc_send, yc_recv, yp_send, yp_recv, yr_send, yr_recv,
    v_send, v_recv, vp_send, vp_recv, o_send, o_recv,
):
    nb, days = ret_ref.shape
    half = w_ref.shape[1] // 2
    quarter = half // 2
    cbits, rbits, mate = peers()

    barrier = pltpu.get_barrier_semaphore()
    for peer in (*cbits, *rbits, mate):
        pl.semaphore_signal(barrier, inc=1, device_id=peer, device_id_type=MESH)

    starts = start_ref[...].reshape(1, nb).astype(F32)
    day = lax.broadcasted_iota(jnp.int32, (days, nb), 0).astype(F32)
    listed = jnp.where(day >= starts, 1.0, 0.0).astype(F32).T
    masked = jnp.where(listed > 0.5, ret_ref[...].astype(F32), 0.0)
    yr[0:nb, :] = masked.astype(BF16)
    yc[0:nb, :] = masked.astype(BF16)
    delta = code_ref[0].astype(F32) / DENOM
    keep = 1.0 - delta

    pl.semaphore_wait(barrier, 7)

    def block(pos, count=1):
        return pl.ds(pos * nb, count * nb)

    def remote(src, dst, send, recv, peer):
        return pltpu.make_async_remote_copy(
            src_ref=src, dst_ref=dst, send_sem=send, recv_sem=recv,
            device_id=peer, device_id_type=MESH)

    def col(m, other=0):
        return block(2 * PLACE[m] + other)

    def yc_copy(to):
        b = last_bit(to)
        return remote(yc.at[col(to - (1 << b))], yc.at[col(to)],
                      yc_send.at[to], yc_recv.at[to], cbits[b])

    def yp_copy(m):
        return remote(yc.at[col(m)], yc.at[col(m, 1)], yp_send.at[m], yp_recv.at[m], mate)

    def yr_copy(to):
        b = last_bit(to)
        return remote(yr.at[block(PLACE[to - (1 << b)])], yr.at[block(PLACE[to])],
                      yr_send.at[to], yr_recv.at[to], rbits[b])

    def v_copy(h, to):
        b = last_bit(to)
        return remote(v.at[h, col(to - (1 << b))], v.at[h, col(to)],
                      v_send.at[h, to], v_recv.at[h, to], cbits[b])

    def vp_copy(h, m):
        return remote(v.at[h, col(m)], v.at[h, col(m, 1)], vp_send.at[h, m], vp_recv.at[h, m], mate)

    def o_copy(q, m):
        return remote(sbuf.at[q, m], rbuf.at[q, m], o_send.at[q, m], o_recv.at[q, m],
                      rbits[ORDERS[q][stage_of(q, m)]])

    def pass_on(copy, m):
        for b in (2, 1, 0):
            if (1 << b) > m:
                copy(m + (1 << b)).start()

    def derive(y_ref, o_ref, s_ref, pos):
        y = y_ref[block(pos), :]
        o_ref[block(pos), :] = jnp.where(y != 0, 1.0, 0.0).astype(BF16)
        s_ref[block(pos), :] = y * y

    have = {"rows": {0}, "cols": {0}, "waited": {0}, "weights": set()}

    def wait_row(m):
        if m not in have["waited"]:
            have["waited"].add(m)
            yr_copy(m).wait_recv()

    def need_tile(side, pair):
        for pos in range(4 * side, 4 * side + 4):
            if pos not in have["rows"]:
                have["rows"].add(pos)
                wait_row(MASKS[pos])
                derive(yr, orow, srow, pos)
        for pos in range(4 * pair, 4 * pair + 4):
            if pos not in have["cols"]:
                have["cols"].add(pos)
                if pos % 2:
                    yp_copy(MASKS[pos // 2]).wait_recv()
                derive(yc, oc, sc, pos)

    def corr_tile(side, pair):
        r = pl.ds(pl.multiple_of(side * 4 * nb, 4 * nb), 4 * nb)
        for k in range(4):
            c = pl.ds(pl.multiple_of(pair * 4 * nb + k * nb, nb), nb)
            cross = lax.dot_general(yr[r, :], yc[c, :], NT, preferred_element_type=F32)
            left = lax.dot_general(srow[r, :], oc[c, :], NT, preferred_element_type=F32)
            right = lax.dot_general(orow[r, :], sc[c, :], NT, preferred_element_type=F32)
            s[r, c] = (cross * lax.rsqrt(left * right + 1e-06) * keep).astype(BF16)

    def need_weights(h):
        if h not in have["weights"]:
            have["weights"].add(h)
            for other in range(8):
                vp_copy(h, other).wait_recv()

    def apply_rows(h, place):
        r = pl.ds(pl.multiple_of(place * nb, nb), nb)
        part[h, place] = jnp.dot(s[r, :], v[h], preferred_element_type=F32)

    def add_up(q, m):
        h, c = q // 2, pl.ds((q % 2) * quarter, quarter)
        k = stage_of(q, m)
        total = part[h, PLACE[m], :, c]
        for b in ORDERS[q][:k]:
            o_copy(q, m | (1 << b)).wait_recv()
            total = total + rbuf[q, m | (1 << b)].astype(F32)
        if k < 3:
            sbuf[q, m] = total.astype(BF16)
            o_copy(q, m).start()
        else:
            out_ref[:, q * quarter:(q + 1) * quarter] = total * sig[...]

    pass_on(yc_copy, 0)
    pass_on(yr_copy, 0)
    yp_copy(0).start()

    seen = jnp.where(masked != 0.0, 1.0, 0.0)
    squared = (masked * masked).astype(BF16)
    orow[0:nb, :] = seen.astype(BF16)
    oc[0:nb, :] = seen.astype(BF16)
    srow[0:nb, :] = squared
    sc[0:nb, :] = squared
    counts = jnp.sum(seen, axis=1, keepdims=True)
    sigma = jnp.sqrt(
        jnp.sum(squared.astype(F32), axis=1, keepdims=True) / jnp.maximum(counts, 1.0) + 1e-06
    )
    scaled = (sigma * w_ref[...].astype(F32)).astype(BF16)
    v[0, 0:nb, :] = scaled[:, :half]
    v[1, 0:nb, :] = scaled[:, half:]
    sig[...] = jnp.broadcast_to(sigma, sig.shape)

    own = block(0)
    cross = lax.dot_general(yr[own, :], yc[own, :], NT, preferred_element_type=F32)
    left = lax.dot_general(srow[own, :], oc[own, :], NT, preferred_element_type=F32)
    right = lax.dot_general(orow[own, :], sc[own, :], NT, preferred_element_type=F32)
    ident = (
        lax.broadcasted_iota(jnp.int32, (nb, nb), 0)
        == lax.broadcasted_iota(jnp.int32, (nb, nb), 1)
    ).astype(F32)
    diag[...] = (cross * lax.rsqrt(left * right + 1e-06) * keep + delta * ident).astype(BF16)

    def event(step):
        what, n = step[0], [int(d) for d in step[1:]]
        if what == "y":
            yc_copy(n[0]).wait_recv()
            pass_on(yc_copy, n[0])
            yp_copy(n[0]).start()
        elif what == "r":
            wait_row(n[0])
            pass_on(yr_copy, n[0])
        elif what == "v":
            h, m = n
            v_copy(h, m).wait_recv()
            pass_on(functools.partial(v_copy, h), m)
            vp_copy(h, m).start()
        elif what == "s":
            v_copy(*n).start()
        elif what == "m":
            vp_copy(n[0], 0).start()
        elif what == "o":
            add_up(*n)

    steps, before = {"T": [], "A": []}, []
    for step in PLAN:
        if step[0] in "TA":
            steps[step[0]].append((tuple(int(d) for d in step[1:]), before))
            before = []
        else:
            before.append(step)

    def entry(i, values):
        out = values[0]
        for k, value in enumerate(values[1:], 1):
            if value != values[k - 1]:
                out = jnp.where(i >= k, value, out)
        return out

    tiles = steps["T"]

    def tile_step(i, carry):
        for k, (where, events) in enumerate(tiles):
            @pl.when(i == k)
            def _(where=where, events=events, k=k):
                for step in events:
                    event(step)
                need_tile(*where)
                if k == 1:
                    s[0:nb, 0:nb] = diag[...]
        corr_tile(entry(i, [w[0] for w, _ in tiles]), entry(i, [w[1] for w, _ in tiles]))
        return carry

    lax.fori_loop(0, len(tiles), tile_step, 0)

    products = steps["A"]

    def product_step(i, carry):
        for k, ((h, m), events) in enumerate(products):
            def prepare(h=h, events=events):
                for step in events:
                    event(step)
                need_weights(h)
            if events or h not in have["weights"]:
                pl.when(i == k)(prepare)
        apply_rows(entry(i, [w[0] for w, _ in products]), entry(i, [PLACE[w[1]] for w, _ in products]))
        return carry

    lax.fori_loop(0, len(products), product_step, 0)
    for step in before:
        event(step)

    for to in range(1, 8):
        yc_copy(to).wait_send()
        yr_copy(to).wait_send()
        for h in (0, 1):
            v_copy(h, to).wait_send()
        for q in range(4):
            o_copy(q, to).wait_send()
    for m in range(8):
        yp_copy(m).wait_send()
        for h in (0, 1):
            vp_copy(h, m).wait_send()


def per_device(returns, start_day, shrink_code, weights):
    nb, days = returns.shape
    port = weights.shape[1]
    half, quarter = port // 2, port // 4
    nr, nc = 8 * nb, 16 * nb
    vmem = pl.BlockSpec(memory_space=pltpu.VMEM)
    smem = pl.BlockSpec(memory_space=pltpu.SMEM)
    dma = pltpu.SemaphoreType.DMA
    return pl.pallas_call(
        kernel,
        out_shape=jax.ShapeDtypeStruct((nb, port), F32),
        in_specs=[vmem, vmem, smem, vmem],
        out_specs=vmem,
        scratch_shapes=[
            pltpu.VMEM((nr, days), BF16), pltpu.VMEM((nr, days), BF16), pltpu.VMEM((nr, days), BF16),
            pltpu.VMEM((nc, days), BF16), pltpu.VMEM((nc, days), BF16), pltpu.VMEM((nc, days), BF16),
            pltpu.VMEM((2, nc, half), BF16),
            pltpu.VMEM((nr, nc), BF16),
            pltpu.VMEM((nb, nb), BF16),
            pltpu.VMEM((nb, quarter), F32),
            pltpu.VMEM((2, 8, nb, half), F32),
            pltpu.VMEM((4, 8, nb, quarter), BF16),
            pltpu.VMEM((4, 8, nb, quarter), BF16),
            dma((8,)), dma((8,)), dma((8,)), dma((8,)), dma((8,)), dma((8,)),
            dma((2, 8)), dma((2, 8)), dma((2, 8)), dma((2, 8)), dma((4, 8)), dma((4, 8)),
        ],
        compiler_params=pltpu.CompilerParams(
            collective_id=0, has_side_effects=True, vmem_limit_bytes=62 << 20
        ),
    )(returns, start_day.reshape(1, nb), shrink_code, weights)


def solution(mesh):
    in_specs = (P(("col", "row"), None), P(("col", "row")), P(), P(("col", "row"), None))
    out_specs = P(("col", "row"), None)
    return jax.shard_map(
        per_device, mesh=mesh, in_specs=in_specs, out_specs=out_specs, check_vma=False
    )
```

time: 522 us -> 57.7 us (0.11)
  waiting for transfers between devices: 375 us -> 0 us
  matrix products: 107 us -> 0 us
  Pallas kernels: 0 us -> 54.4 us
  other arithmetic: 16.9 us -> 0 us
  between operations: 14.2 us -> 0.66 us
    reduce_scatter x2 -> x0, waiting for transfers between devices: 193 us -> none  [the longest x1 108 us: per_device(): row_part = lax.psum_scatter(terms, 'col', scatter_dimension=0, tiled=True)]
    all_gather x4 -> x0, waiting for transfers between devices: 181 us -> none  [the longest x1 50 us: per_device(): row_v = lax.all_gather(scaled, 'col', axis=0, tiled=True)]
    dot_general x43 -> x0, matrix products: 107 us -> none  [the longest x7 33.3 us: step(): mirror = jnp.dot(shrunk.T, piece_v, preferred_element_type=jnp.float32)]
    pallas_call x0 -> x1, Pallas kernels: none -> 54.4 us  [per_device(): pl.pallas_call(kernel, out_shape=jax.ShapeDtypeStruct((nb, port), F32), i...]
    add x2 -> x0, other arithmetic: 6.44 us -> none  [the longest x1 6.44 us: per_device(): col_acc = col_acc + opp_mirror]
  transfers between devices with their start and end apart: 6 -> 0, of which waited for: 6 -> 0; matrix products, arithmetic and copies ran while one was open for 4% -> 0% of each run, Pallas kernels for 0% -> 0%
where the time goes in v2:
time: 57.7 us; the launch traced here: 56.9 us
  Pallas kernels  54.4 us (94%)
  local copies, waits for them, and re-layouts  1.87 us (3%)
  between operations  0.66 us (1%)
    pallas_call x1, Pallas kernels, per_device(): pl.pallas_call(kernel, out_shape=jax.ShapeDtypeStruct((nb, port), F32), i...  54.4 us
    unnamed x1, local copies, waits for them, and re-layouts  1.87 us

profile of v2, /device:TPU:0, one launch (start us, length us, event | category | flops | bytes accessed | tf_op | source)
XLA Modules:
  0.0 56.9 jit_solution(9693682016746602589)
XLA Ops:
  0.7 54.4 %shard_map.46 = f32[256,512]{1,0:T(8,128)} custom-call(bf16[256,256]{1,0:T(8,128)(2,1)} %ret_ref.1, s32[1,256]{1,0:T(1,128)} %bitcast.1, s32[1]{0:T(128)S(6)} %copy.6.code_ref, bf16[256,512]{1,0:T(8,128)(2,1)} %w_ref.1), custom_call_target="tpu_custom_call" | custom-call | tf_op jit(solution)/shard_map/pallas_call | solution.py:333
  55.0 1.9 %copy.7 = f32[256,512]{1,0:T(8,128)} copy(f32[256,512]{1,0:T(8,128)} %shard_map.46) | data formatting | bytes 1048576

commit v3 on v2

--- a/solution.py
+++ b/solution.py
@@ -16,33 +16,33 @@
 MASKS = (0, 1, 2, 4, 3, 5, 6, 7)
 PLACE = tuple(MASKS.index(m) for m in range(8))
 
-ORDERS = ((0, 1, 2), (1, 2, 0), (2, 0, 1), (2, 1, 0))
+ORDERS = ((1, 2, 0), (2, 0, 1), (2, 0, 1), (2, 1, 0))
 PLAN = (
-    "s01", "s11", "s12", "y1", "r1", "r2", "y4", "s02", "v01", "y2", "T00",
-    "v11", "v12", "T01",
-    "r3", "v05", "y3", "y5", "T02",
-    "s04", "v02", "T12",
-    "v03", "m1", "s14", "T11",
-    "v15", "y7", "y6", "T10",
-    "v04", "v13", "T13",
-    "v16", "v06", "v07", "m0", "T03",
-    "A05",
-    "v17", "v14", "o05", "A07",
-    "o17", "o07", "A03",
-    "o13", "o03", "A17",
-    "o37", "o27", "A06",
-    "o16", "A15",
-    "o25", "o35", "A16",
-    "o36", "o06", "A13",
-    "o15", "A02",
-    "o33", "o26", "A04",
-    "o23", "A01",
-    "o12", "o14", "A11",
-    "o02", "o01", "o21", "A14",
-    "o11", "A00",
-    "A12",
-    "o32", "o24", "o04", "o22", "A10",
-    "o34", "o31", "o00", "o10", "o20", "o30",
+    "s02", "s01", "s11", "y01", "r01", "y14", "y02", "r11", "r02", "r12", "y11", "v01", "y04", "y12", "y03", "s14", "r03", "s12", "r13", "T00",
+    "y13", "m1", "s04", "y15", "T01",
+    "v03", "v11", "y06", "v02", "y16", "T11",
+    "y07", "y05", "y17", "m0", "T10",
+    "v12", "T13",
+    "v05", "v13", "v04", "T12",
+    "v15", "v06", "v07", "T03",
+    "v16", "A03",
+    "v14", "v17", "A07",
+    "o17", "A06",
+    "o16", "A05",
+    "o15", "A16",
+    "o26", "A17",
+    "o37", "o27", "o07", "A13",
+    "o36", "o06", "A15",
+    "o13", "o03", "o35", "T02",
+    "o25", "A02",
+    "o02", "o23", "o05", "A04",
+    "o14", "o33", "A14",
+    "o24", "A12",
+    "o12", "o04", "o34", "A11",
+    "o21", "A10",
+    "o32", "A01",
+    "o01", "A00",
+    "o22", "o11", "o31", "o00", "o10", "o20", "o30",
 )
 
 
@@ -121,21 +121,28 @@
             src_ref=src, dst_ref=dst, send_sem=send, recv_sem=recv,
             device_id=peer, device_id_type=MESH)
 
+    def col_place(m, other=0):
+        return 8 * (PLACE[m] // 4) + 4 * other + PLACE[m] % 4
+
     def col(m, other=0):
-        return block(2 * PLACE[m] + other)
-
-    def yc_copy(to):
+        return block(col_place(m, other))
+
+    def piece(place, g):
+        return pl.ds(place * nb + g * (nb // 2), nb // 2)
+
+    def yc_copy(g, to):
         b = last_bit(to)
-        return remote(yc.at[col(to - (1 << b))], yc.at[col(to)],
-                      yc_send.at[to], yc_recv.at[to], cbits[b])
-
-    def yp_copy(m):
-        return remote(yc.at[col(m)], yc.at[col(m, 1)], yp_send.at[m], yp_recv.at[m], mate)
-
-    def yr_copy(to):
+        return remote(yc.at[piece(col_place(to - (1 << b)), g)], yc.at[piece(col_place(to), g)],
+                      yc_send.at[g, to], yc_recv.at[g, to], cbits[b])
+
+    def yp_copy(g, m):
+        return remote(yc.at[piece(col_place(m), g)], yc.at[piece(col_place(m, 1), g)],
+                      yp_send.at[g, m], yp_recv.at[g, m], mate)
+
+    def yr_copy(g, to):
         b = last_bit(to)
-        return remote(yr.at[block(PLACE[to - (1 << b)])], yr.at[block(PLACE[to])],
-                      yr_send.at[to], yr_recv.at[to], rbits[b])
+        return remote(yr.at[piece(PLACE[to - (1 << b)], g)], yr.at[piece(PLACE[to], g)],
+                      yr_send.at[g, to], yr_recv.at[g, to], rbits[b])
 
     def v_copy(h, to):
         b = last_bit(to)
@@ -159,24 +166,26 @@
         o_ref[block(pos), :] = jnp.where(y != 0, 1.0, 0.0).astype(BF16)
         s_ref[block(pos), :] = y * y
 
-    have = {"rows": {0}, "cols": {0}, "waited": {0}, "weights": set()}
-
-    def wait_row(m):
-        if m not in have["waited"]:
-            have["waited"].add(m)
-            yr_copy(m).wait_recv()
+    have = {"rows": {0}, "cols": {0}, "waited": {(0, 0), (1, 0)}, "weights": set()}
+
+    def wait_row(g, m):
+        if (g, m) not in have["waited"]:
+            have["waited"].add((g, m))
+            yr_copy(g, m).wait_recv()
 
     def need_tile(side, pair):
         for pos in range(4 * side, 4 * side + 4):
             if pos not in have["rows"]:
                 have["rows"].add(pos)
-                wait_row(MASKS[pos])
+                wait_row(0, MASKS[pos])
+                wait_row(1, MASKS[pos])
                 derive(yr, orow, srow, pos)
         for pos in range(4 * pair, 4 * pair + 4):
             if pos not in have["cols"]:
                 have["cols"].add(pos)
-                if pos % 2:
-                    yp_copy(MASKS[pos // 2]).wait_recv()
+                if pos // 4 % 2:
+                    for g in (0, 1):
+                        yp_copy(g, MASKS[4 * (pos // 8) + pos % 4]).wait_recv()
                 derive(yc, oc, sc, pos)
 
     def corr_tile(side, pair):
@@ -211,9 +220,10 @@
         else:
             out_ref[:, q * quarter:(q + 1) * quarter] = total * sig[...]
 
-    pass_on(yc_copy, 0)
-    pass_on(yr_copy, 0)
-    yp_copy(0).start()
+    for g in (0, 1):
+        pass_on(functools.partial(yc_copy, g), 0)
+        yp_copy(g, 0).start()
+        pass_on(functools.partial(yr_copy, g), 0)
 
     seen = jnp.where(masked != 0.0, 1.0, 0.0)
     squared = (masked * masked).astype(BF16)
@@ -243,12 +253,12 @@
     def event(step):
         what, n = step[0], [int(d) for d in step[1:]]
         if what == "y":
-            yc_copy(n[0]).wait_recv()
-            pass_on(yc_copy, n[0])
-            yp_copy(n[0]).start()
+            yc_copy(*n).wait_recv()
+            pass_on(functools.partial(yc_copy, n[0]), n[1])
+            yp_copy(*n).start()
         elif what == "r":
-            wait_row(n[0])
-            pass_on(yr_copy, n[0])
+            wait_row(*n)
+            pass_on(functools.partial(yr_copy, n[0]), n[1])
         elif what == "v":
             h, m = n
             v_copy(h, m).wait_recv()
@@ -261,10 +271,12 @@
         elif what == "o":
             add_up(*n)
 
-    steps, before = {"T": [], "A": []}, []
+    runs, before = [], []
     for step in PLAN:
         if step[0] in "TA":
-            steps[step[0]].append((tuple(int(d) for d in step[1:]), before))
+            if not runs or runs[-1][0] != step[0]:
+                runs.append((step[0], []))
+            runs[-1][1].append((tuple(int(d) for d in step[1:]), before))
             before = []
         else:
             before.append(step)
@@ -276,49 +288,45 @@
                 out = jnp.where(i >= k, value, out)
         return out
 
-    tiles = steps["T"]
-
-    def tile_step(i, carry):
-        for k, (where, events) in enumerate(tiles):
-            @pl.when(i == k)
-            def _(where=where, events=events, k=k):
-                for step in events:
-                    event(step)
-                need_tile(*where)
-                if k == 1:
-                    s[0:nb, 0:nb] = diag[...]
-        corr_tile(entry(i, [w[0] for w, _ in tiles]), entry(i, [w[1] for w, _ in tiles]))
-        return carry
-
-    lax.fori_loop(0, len(tiles), tile_step, 0)
-
-    products = steps["A"]
-
-    def product_step(i, carry):
-        for k, ((h, m), events) in enumerate(products):
-            def prepare(h=h, events=events):
-                for step in events:
-                    event(step)
-                need_weights(h)
-            if events or h not in have["weights"]:
+    def run_steps(kind, entries, first):
+        firsts = [e[0] for e, _ in entries]
+        seconds = [e[1] if kind == "T" else PLACE[e[1]] for e, _ in entries]
+
+        def one(i, carry):
+            for k, (where, events) in enumerate(entries):
+                def prepare(where=where, events=events, k=k):
+                    for step in events:
+                        event(step)
+                    if kind == "T":
+                        need_tile(*where)
+                    else:
+                        need_weights(where[0])
+                    if first and k == 1:
+                        s[0:nb, 0:nb] = diag[...]
                 pl.when(i == k)(prepare)
-        apply_rows(entry(i, [w[0] for w, _ in products]), entry(i, [PLACE[w[1]] for w, _ in products]))
-        return carry
-
-    lax.fori_loop(0, len(products), product_step, 0)
+            if kind == "T":
+                corr_tile(entry(i, firsts), entry(i, seconds))
+            else:
+                apply_rows(entry(i, firsts), entry(i, seconds))
+            return carry
+
+        lax.fori_loop(0, len(entries), one, 0)
+
+    for n, (kind, entries) in enumerate(runs):
+        run_steps(kind, entries, n == 0)
     for step in before:
         event(step)
 
     for to in range(1, 8):
-        yc_copy(to).wait_send()
-        yr_copy(to).wait_send()
         for h in (0, 1):
+            yc_copy(h, to).wait_send()
+            yr_copy(h, to).wait_send()
             v_copy(h, to).wait_send()
         for q in range(4):
             o_copy(q, to).wait_send()
     for m in range(8):
-        yp_copy(m).wait_send()
         for h in (0, 1):
+            yp_copy(h, m).wait_send()
             vp_copy(h, m).wait_send()
 
 
@@ -345,7 +353,7 @@
             pltpu.VMEM((2, 8, nb, half), F32),
             pltpu.VMEM((4, 8, nb, quarter), BF16),
             pltpu.VMEM((4, 8, nb, quarter), BF16),
-            dma((8,)), dma((8,)), dma((8,)), dma((8,)), dma((8,)), dma((8,)),
+            dma((2, 8)), dma((2, 8)), dma((2, 8)), dma((2, 8)), dma((2, 8)), dma((2, 8)),
             dma((2, 8)), dma((2, 8)), dma((2, 8)), dma((2, 8)), dma((4, 8)), dma((4, 8)),
         ],
         compiler_params=pltpu.CompilerParams(

time: 57.7 us -> 57.9 us (level); the launches traced: 56.9 us -> 57.7 us
  Pallas kernels: 54.4 us -> 55.2 us
    pallas_call x1, Pallas kernels: 54.4 us -> 55.2 us  [per_device(): pl.pallas_call(kernel, out_shape=jax.ShapeDtypeStruct((nb, port), F32), i...]
where the time goes in v3:
time: 57.9 us; the launch traced here: 57.7 us
  Pallas kernels  55.2 us (95%)
  local copies, waits for them, and re-layouts  1.87 us (3%)
  between operations  0.66 us (1%)
    pallas_call x1, Pallas kernels, per_device(): pl.pallas_call(kernel, out_shape=jax.ShapeDtypeStruct((nb, port), F32), i...  55.2 us
    unnamed x1, local copies, waits for them, and re-layouts  1.87 us

profile of v3, /device:TPU:0, one launch (start us, length us, event | category | flops | bytes accessed | tf_op | source)
XLA Modules:
  0.0 57.7 jit_solution(4277471641915773689)
XLA Ops:
  0.7 55.2 %shard_map.46 = f32[256,512]{1,0:T(8,128)} custom-call(bf16[256,256]{1,0:T(8,128)(2,1)} %ret_ref.1, s32[1,256]{1,0:T(1,128)} %bitcast.1, s32[1]{0:T(128)S(6)} %copy.6.code_ref, bf16[256,512]{1,0:T(8,128)(2,1)} %w_ref.1), custom_call_target="tpu_custom_call" | custom-call | tf_op jit(solution)/shard_map/pallas_call | solution.py:341
  55.9 1.9 %copy.7 = f32[256,512]{1,0:T(8,128)} copy(f32[256,512]{1,0:T(8,128)} %shard_map.46) | data formatting | bytes 1048576

commit v4 on v2

--- a/solution.py
+++ b/solution.py
@@ -68,7 +68,7 @@
         return tuple(a * (1 - core) + b * core for a, b in zip(first, second))
 
     out = []
-    for flip in (flip1, flip3):
+    for flip in (flip3, flip1):
         along_x = device(flip(x), y, z, core)
         along_y = device(x, flip(y), z, core)
         along_z = device(x, y, flip(z), core)

time: 57.7 us -> 56.2 us (0.974); the launches traced: 56.9 us -> 56.1 us
  Pallas kernels: 54.4 us -> 53.5 us
    pallas_call x1, Pallas kernels: 54.4 us -> 53.5 us  [per_device(): pl.pallas_call(kernel, out_shape=jax.ShapeDtypeStruct((nb, port), F32), i...]
where the time goes in v4:
time: 56.2 us; the launch traced here: 56.1 us
  Pallas kernels  53.5 us (95%)
  local copies, waits for them, and re-layouts  1.87 us (3%)
  between operations  0.66 us (1%)
    pallas_call x1, Pallas kernels, per_device(): pl.pallas_call(kernel, out_shape=jax.ShapeDtypeStruct((nb, port), F32), i...  53.5 us
    unnamed x1, local copies, waits for them, and re-layouts  1.87 us

profile of v4, /device:TPU:0, one launch (start us, length us, event | category | flops | bytes accessed | tf_op | source)
XLA Modules:
  0.0 56.1 jit_solution(4747885327504682876)
XLA Ops:
  0.7 53.5 %shard_map.46 = f32[256,512]{1,0:T(8,128)} custom-call(bf16[256,256]{1,0:T(8,128)(2,1)} %ret_ref.1, s32[1,256]{1,0:T(1,128)} %bitcast.1, s32[1]{0:T(128)S(6)} %copy.6.code_ref, bf16[256,512]{1,0:T(8,128)(2,1)} %w_ref.1), custom_call_target="tpu_custom_call" | custom-call | tf_op jit(solution)/shard_map/pallas_call | solution.py:333
  54.2 1.9 %copy.7 = f32[256,512]{1,0:T(8,128)} copy(f32[256,512]{1,0:T(8,128)} %shard_map.46) | data formatting | bytes 1048576

commit v5 on v4

--- a/solution.py
+++ b/solution.py
@@ -88,15 +88,17 @@
 
 
 def kernel(
-    ret_ref, start_ref, code_ref, w_ref, out_ref,
+    ret_ref, start_ref, code_ref, w_hbm, out_ref,
     yr, orow, srow, yc, oc, sc, v, s, diag, sig, part, sbuf, rbuf,
     yc_send, yc_recv, yp_send, yp_recv, yr_send, yr_recv,
-    v_send, v_recv, vp_send, vp_recv, o_send, o_recv,
+    v_send, v_recv, vp_send, vp_recv, o_send, o_recv, w_ref, w_sem,
 ):
     nb, days = ret_ref.shape
     half = w_ref.shape[1] // 2
     quarter = half // 2
     cbits, rbits, mate = peers()
+    w_copy = pltpu.make_async_copy(w_hbm, w_ref, w_sem)
+    w_copy.start()
 
     barrier = pltpu.get_barrier_semaphore()
     for peer in (*cbits, *rbits, mate):
@@ -225,6 +227,7 @@
     sigma = jnp.sqrt(
         jnp.sum(squared.astype(F32), axis=1, keepdims=True) / jnp.maximum(counts, 1.0) + 1e-06
     )
+    w_copy.wait()
     scaled = (sigma * w_ref[...].astype(F32)).astype(BF16)
     v[0, 0:nb, :] = scaled[:, :half]
     v[1, 0:nb, :] = scaled[:, half:]
@@ -333,7 +336,7 @@
     return pl.pallas_call(
         kernel,
         out_shape=jax.ShapeDtypeStruct((nb, port), F32),
-        in_specs=[vmem, vmem, smem, vmem],
+        in_specs=[vmem, vmem, smem, pl.BlockSpec(memory_space=pl.ANY)],
         out_specs=vmem,
         scratch_shapes=[
             pltpu.VMEM((nr, days), BF16), pltpu.VMEM((nr, days), BF16), pltpu.VMEM((nr, days), BF16),
@@ -347,6 +350,7 @@
             pltpu.VMEM((4, 8, nb, quarter), BF16),
             dma((8,)), dma((8,)), dma((8,)), dma((8,)), dma((8,)), dma((8,)),
             dma((2, 8)), dma((2, 8)), dma((2, 8)), dma((2, 8)), dma((4, 8)), dma((4, 8)),
+            pltpu.VMEM((nb, port), BF16), dma,
         ],
         compiler_params=pltpu.CompilerParams(
             collective_id=0, has_side_effects=True, vmem_limit_bytes=62 << 20

time: 56.2 us -> 56.1 us (level)
  no operation moved by 1% of the time
where the time goes in v5:
time: 56.1 us; the launch traced here: 56 us
  Pallas kernels  53.4 us (95%)
  local copies, waits for them, and re-layouts  1.87 us (3%)
  between operations  0.66 us (1%)
    pallas_call x1, Pallas kernels, per_device(): pl.pallas_call(kernel, out_shape=jax.ShapeDtypeStruct((nb, port), F32), i...  53.4 us
    unnamed x1, local copies, waits for them, and re-layouts  1.87 us

profile of v5, /device:TPU:0, one launch (start us, length us, event | category | flops | bytes accessed | tf_op | source)
XLA Modules:
  0.0 56.0 jit_solution(2215895350497031650)
XLA Ops:
  0.7 53.4 %shard_map.46 = f32[256,512]{1,0:T(8,128)} custom-call(bf16[256,256]{1,0:T(8,128)(2,1)} %ret_ref.1, s32[1,256]{1,0:T(1,128)} %bitcast.1, s32[1]{0:T(128)S(6)} %copy.6.code_ref, bf16[256,512]{1,0:T(8,128)(2,1)} %w_hbm.1), custom_call_target="tpu_custom_call" | custom-call | tf_op jit(solution)/shard_map/pallas_call | solution.py:336
  54.1 1.9 %copy.7 = f32[256,512]{1,0:T(8,128)} copy(f32[256,512]{1,0:T(8,128)} %shard_map.46) | data formatting | bytes 1048576
